TPU v7x, 128 devices: a whole 4x4x4 slice. The times are simulated.
128 devices in a mesh: node: 4 (over y_hi, core), hst: 32 (over y_lo, x, z).
Axes of the slice: x: 4, y: 4 (y_hi: 2, y_lo: 2; y = y_hi * 2 + y_lo), z: 4, core: 2. Of those that a mesh axis runs over, the one named last changes fastest.
Arguments:
- hidden: bfloat16 [32, 4096, 640], P('hst', 'node'), may hold values from -6 to 6
- cotangent: bfloat16 [32, 4096, 4608], P('hst', 'node'), may hold values from -12 to 12
- anchor: float32 [32, 640, 4608], P('hst', 'node'), may hold values from -0.25 to 0.25
- momentum: float32 [32, 640, 4608], P('hst', 'node'), may hold values from -0.6 to 0.6
- round_mask: int32 [1], replicated, may hold values from 1 to 31
Outputs:
- weights_out: bfloat16 [32, 640, 4608], P('hst')
- momentum_out: float32 [32, 640, 4608], P('hst', 'node')
Inputs may be any that keep to these rules, and one draw needn't show every extreme that they name: round_mask is the same for all hosts; host i averages with the hosts i XOR s for every s whose bits lie within round_mask.
All inputs are finite; a program needn't handle non-finite values.
Results may differ from a plain program's by a relative error of at most 0.009.
Values may be sent and summed in bfloat16 or wider, within the bound.
A program may use at most 256 MiB of HBM per device.

v0:
```python
import jax
import jax.numpy as jnp
from jax import lax
from jax.sharding import PartitionSpec as P

base_rate = 0.5
slow_rate = 1.0
slow_beta = 0.7


def swapped(block, axis, bit):
    count = lax.axis_size(axis)
    route = []
    for low in range(count):
        high = low | 1 << bit
        if high != low and high < count:
            route += [(low, high), (high, low)]
    return lax.ppermute(block, axis, route)


def half_step(current, bit_index):
    other_rows = swapped(current.astype(jnp.bfloat16), "hst", bit_index).astype(current.dtype)
    return 0.5 * (current + other_rows)


def local(hidden, cotangent, anchor, momentum, round_mask):
    tokens_here = hidden[0]
    grads_in = cotangent[0]
    token_scale = 1.0 / (tokens_here.shape[0] * lax.axis_size("node"))
    product = lax.dot_general(
        tokens_here, grads_in, (((0,), (0,)), ((), ())), preferred_element_type=jnp.float32
    )
    gradient = lax.psum_scatter(
        (product * token_scale).astype(jnp.bfloat16), "node", scatter_dimension=0, tiled=True
    ).astype(jnp.float32)
    stepped = anchor[0] - base_rate * gradient
    mask_value = round_mask[0]
    host_count = lax.axis_size("hst")
    bit_count = host_count.bit_length() - 1
    bit_list = list(range(bit_count))
    averaged = stepped
    for bit_index in bit_list:
        active = jnp.bitwise_and(jnp.right_shift(mask_value, bit_index), 1) == 1
        averaged = jnp.where(active, half_step(averaged, bit_index), averaged)
    momentum_new = slow_beta * momentum[0] + (anchor[0] - averaged) / base_rate
    updated = (anchor[0] - slow_rate * base_rate * momentum_new).astype(jnp.bfloat16)
    weights_whole = lax.all_gather(updated[None], "node", axis=1, tiled=True)
    return (weights_whole, momentum_new[None])


def solution(mesh):
    placed = (
        P("hst", "node", None),
        P("hst", "node", None),
        P("hst", "node", None),
        P("hst", "node", None),
        P(),
    )
    return jax.shard_map(
        local,
        mesh=mesh,
        in_specs=placed,
        out_specs=(P("hst", None, None), P("hst", "node", None)),
        check_vma=False,
    )
```

profile of v0, /device:TPU:1, one launch (start us, length us, event | category | flops | bytes accessed | tf_op | source)
XLA Modules:
  0.0 318.9 jit_solution(657283550039399668)
XLA Ops:
  7.2 0.0 copy-start
  7.2 0.0 reduce-scatter.2.cloned.1.call-start
  7.2 1.3 copy-done
  8.5 10.5 %multiply_convert_fusion = bf16[640,4608]{1,0:T(8,128)(2,1)} fusion(bf16[1,1024,4608]{2,1,0:T(8,128)(2,1)} %param.6, bf16[1,1024,640]{2,1,0:T(8,128)(2,1)S(1)} %copy-done), kind=kOutput, calls=%fused_computation | convolution fusion | flops 6045696000 | bytes 16646144 | tf_op jit(solution)/shard_map/dot_general | solution.py:30
  19.0 0.0 reduce-scatter.2.cloned.1.call-update
  19.0 0.0 all-gather.3.cloned.1.call-start
  19.0 66.0 %reduce-scatter.2.cloned.1.call-done = bf16[160,4608]{1,0:T(8,128)(2,1)} async-done(((bf16[640,4608]{1,0:T(8,128)(2,1)}), bf16[160,4608]{1,0:T(8,128)(2,1)}) %reduce-scatter.2.cloned.1.call-update) | async-done | bytes 1474576 | tf_op jit(solution)/shard_map/reduce_scatter | solution.py:33
  85.0 0.0 copy-start.1
  85.0 0.0 copy-start.2
  85.0 2.8 fusion.6
  87.8 1.3 collective-permute-start
  89.8 31.2 %collective-permute-done = bf16[160,4608]{1,0:T(8,128)(2,1)S(1)} collective-permute-done((bf16[160,4608]{1,0:T(8,128)(2,1)S(1)}, bf16[160,4608]{1,0:T(8,128)(2,1)S(1)}, u32[]{:S(2)}, u32[]{:S(2)}) %collective-permute-start) | collective-permute-done | bytes 1474592 | tf_op jit(solution)/shard_map/ppermute | solution.py:18
  121.1 0.0 copy-done.1
  121.1 0.0 copy-done.2
  121.1 0.7 fusion.11
  121.8 2.9 collective-permute-start.1
  124.7 30.9 %collective-permute-done.1 = bf16[160,4608]{1,0:T(8,128)(2,1)S(1)} collective-permute-done((bf16[160,4608]{1,0:T(8,128)(2,1)S(1)}, bf16[160,4608]{1,0:T(8,128)(2,1)S(1)}, u32[]{:S(2)}, u32[]{:S(2)}) %collective-permute-start.1) | collective-permute-done | bytes 1474592 | tf_op jit(solution)/shard_map/ppermute | solution.py:18
  155.6 0.4 fusion.7
  156.0 1.2 collective-permute-start.2
  157.3 30.2 %collective-permute-done.2 = bf16[160,4608]{1,0:T(8,128)(2,1)S(1)} collective-permute-done((bf16[160,4608]{1,0:T(8,128)(2,1)S(1)}, bf16[160,4608]{1,0:T(8,128)(2,1)S(1)}, u32[]{:S(2)}, u32[]{:S(2)}) %collective-permute-start.2) | collective-permute-done | bytes 1474592 | tf_op jit(solution)/shard_map/ppermute | solution.py:18
  187.4 0.8 fusion.10
  188.3 2.7 collective-permute-start.3
  191.0 29.2 %collective-permute-done.3 = bf16[160,4608]{1,0:T(8,128)(2,1)S(1)} collective-permute-done((bf16[160,4608]{1,0:T(8,128)(2,1)S(1)}, bf16[160,4608]{1,0:T(8,128)(2,1)S(1)}, u32[]{:S(2)}, u32[]{:S(2)}) %collective-permute-start.3) | collective-permute-done | bytes 1474592 | tf_op jit(solution)/shard_map/ppermute | solution.py:18
  220.2 0.0 copy-start.3
  220.2 0.4 fusion.8
  220.7 0.3 collective-permute-start.4
  221.0 29.2 %collective-permute-done.4 = bf16[160,4608]{1,0:T(8,128)(2,1)S(1)} collective-permute-done((bf16[160,4608]{1,0:T(8,128)(2,1)S(1)}, bf16[160,4608]{1,0:T(8,128)(2,1)S(1)}, u32[]{:S(2)}, u32[]{:S(2)}) %collective-permute-start.4) | collective-permute-done | bytes 1474592 | tf_op jit(solution)/shard_map/ppermute | solution.py:18
  250.2 0.0 copy-done.3
  250.2 3.5 %fusion.5 = (bf16[160,4608]{1,0:T(8,128)(2,1)}, f32[160,4608]{1,0:T(8,128)}) fusion(f32[1,160,4608]{2,1,0:T(8,128)S(1)} %copy-done.1, bf16[160,4608]{1,0:T(8,128)(2,1)S(1)} %collective-permute-done.4, f32[160,4608]{1,0:T(8,128)S(1)} %get-tuple-element.5, bf16[160,4608]{1,0:T(8,128)(2,1)S(1)} %collective-permute-done.3, pred[]{:T(512)} %bitcast.3, ...), kind=kLoop, calls=%fused_computation.8 | loop fusion | flops 11059200 | bytes 16220162 | tf_op jit(solution)/shard_map/convert_element_type | solution.py:46
  253.7 0.0 all-gather.3.cloned.1.call-update
  253.7 52.7 %all-gather.3.cloned.1.call-done = bf16[640,4608]{1,0:T(8,128)(2,1)} async-done(((bf16[160,4608]{1,0:T(8,128)(2,1)}), bf16[640,4608]{1,0:T(8,128)(2,1)}) %all-gather.3.cloned.1.call-update) | async-done | bytes 5898256 | tf_op jit(solution)/shard_map/all_gather | solution.py:47
  306.4 5.6 %copy.9 = bf16[1,640,4608]{2,1,0:T(8,128)(2,1)} copy(bf16[1,640,4608]{2,1,0:T(8,128)(2,1)} %bitcast.34) | data formatting | bytes 11796480
Async XLA Ops:
  7.2 1.3 copy-start
  7.2 77.9 %reduce-scatter.2.cloned.1.call-start = ((), (), s32[]{:S(2)}) async-start(), calls=%async_computation.1 | async-start | bytes 7372800 | tf_op jit(solution)/shard_map/reduce_scatter | solution.py:33
  19.0 287.4 %all-gather.3.cloned.1.call-start = ((), (), s32[]{:S(2)}) async-start(), calls=%async_computation.2 | async-start | bytes 7372800 | tf_op jit(solution)/shard_map/all_gather | solution.py:47
  85.0 36.0 %copy-start.1 = (f32[1,160,4608]{2,1,0:T(8,128)S(1)}, f32[1,160,4608]{2,1,0:T(8,128)}, u32[]{:S(2)}) copy-start(f32[1,160,4608]{2,1,0:T(8,128)} %param.7) | copy-start | bytes 8847364
  85.0 36.0 %copy-start.2 = (bf16[160,4608]{1,0:T(8,128)(2,1)S(1)}, bf16[160,4608]{1,0:T(8,128)(2,1)}, u32[]{:S(2)}) copy-start(bf16[160,4608]{1,0:T(8,128)(2,1)} %reduce-scatter.2.cloned.1.call-done) | copy-start | bytes 4423684
  87.8 33.2 %collective-permute-start = (bf16[160,4608]{1,0:T(8,128)(2,1)S(1)}, bf16[160,4608]{1,0:T(8,128)(2,1)S(1)}, u32[]{:S(2)}, u32[]{:S(2)}) collective-permute-start(bf16[160,4608]{1,0:T(8,128)(2,1)S(1)} %fusion.6), channel_id=1, source_target_pairs={{0,1},{1,0},{2,3},{3,2},{4,5},{5,4},{6,7},{7,6},{8,9},{9,8},{10,11... | collective-permute-start | bytes 4423688 | tf_op jit(solution)/shard_map/ppermute | solution.py:18
  121.8 33.8 %collective-permute-start.1 = (bf16[160,4608]{1,0:T(8,128)(2,1)S(1)}, bf16[160,4608]{1,0:T(8,128)(2,1)S(1)}, u32[]{:S(2)}, u32[]{:S(2)}) collective-permute-start(bf16[160,4608]{1,0:T(8,128)(2,1)S(1)} %get-tuple-element.6), channel_id=1, source_target_pairs={{0,2},{2,0},{1,3},{3,1},{4,6},{6,4},{5,7},{7,5},{8,10},{10,8},{9,1... | collective-permute-start | bytes 4423688 | tf_op jit(solution)/shard_map/ppermute | solution.py:18
  156.0 31.4 %collective-permute-start.2 = (bf16[160,4608]{1,0:T(8,128)(2,1)S(1)}, bf16[160,4608]{1,0:T(8,128)(2,1)S(1)}, u32[]{:S(2)}, u32[]{:S(2)}) collective-permute-start(bf16[160,4608]{1,0:T(8,128)(2,1)S(1)} %fusion.7), channel_id=1, source_target_pairs={{0,4},{4,0},{1,5},{5,1},{2,6},{6,2},{3,7},{7,3},{8,12},{12,8},{9,1... | collective-permute-start | bytes 4423688 | tf_op jit(solution)/shard_map/ppermute | solution.py:18
  188.3 32.0 %collective-permute-start.3 = (bf16[160,4608]{1,0:T(8,128)(2,1)S(1)}, bf16[160,4608]{1,0:T(8,128)(2,1)S(1)}, u32[]{:S(2)}, u32[]{:S(2)}) collective-permute-start(bf16[160,4608]{1,0:T(8,128)(2,1)S(1)} %get-tuple-element.4), channel_id=1, source_target_pairs={{0,8},{8,0},{1,9},{9,1},{2,10},{10,2},{3,11},{11,3},{4,12},{12,4},... | collective-permute-start | bytes 4423688 | tf_op jit(solution)/shard_map/ppermute | solution.py:18
  220.2 30.0 %copy-start.3 = (f32[1,160,4608]{2,1,0:T(8,128)S(1)}, f32[1,160,4608]{2,1,0:T(8,128)}, u32[]{:S(2)}) copy-start(f32[1,160,4608]{2,1,0:T(8,128)} %param.8) | copy-start | bytes 8847364
  220.7 29.6 %collective-permute-start.4 = (bf16[160,4608]{1,0:T(8,128)(2,1)S(1)}, bf16[160,4608]{1,0:T(8,128)(2,1)S(1)}, u32[]{:S(2)}, u32[]{:S(2)}) collective-permute-start(bf16[160,4608]{1,0:T(8,128)(2,1)S(1)} %fusion.8), channel_id=1, source_target_pairs={{0,16},{16,0},{1,17},{17,1},{2,18},{18,2},{3,19},{19,3},{4,20},{20... | collective-permute-start | bytes 4423688 | tf_op jit(solution)/shard_map/ppermute | solution.py:18
Sparse Core Ops, SparseCore 0:
  19.1 65.8 reduce-scatter.1
  253.8 52.5 all-gather.2
where the time goes:
time: 319 us
  waiting for transfers between devices  269 us (84%)
  between operations  14.7 us (5%)
  matrix products  10.5 us (3%)
  starting transfers between devices  8.68 us (3%)
  other arithmetic  8.62 us (3%)
  local copies, waits for them, and re-layouts  6.9 us (2%)
    ppermute x5, waiting for transfers between devices, swapped(): return lax.ppermute(block, axis, route)  151 us
    reduce_scatter x1, waiting for transfers between devices, local(): lax.psum_scatter((product * token_scale).astype(jnp.bfloat16), 'node', sc...  66 us
    all_gather x1, waiting for transfers between devices, local(): weights_whole = lax.all_gather(updated[None], 'node', axis=1, tiled=True)  52.7 us
    dot_general x1, matrix products, local(): lax.dot_general(tokens_here, grads_in, (((0,), (0,)), ((), ())), preferre...  10.5 us
    ppermute x5, starting transfers between devices, swapped(): return lax.ppermute(block, axis, route)  8.6 us
    unnamed x9, local copies, waits for them, and re-layouts  6.9 us
  transfers between devices with their start and end apart: 7, of which 7 were waited for; matrix products, arithmetic and copies ran while one was open for 0% of the time, Pallas kernels for 0%

commit v1 on v0

v1 whole, which is shorter than its diff:
```python
import functools

import jax
import jax.numpy as jnp
from jax import lax
from jax.experimental import pallas as pl
from jax.experimental.pallas import tpu as pltpu
from jax.sharding import PartitionSpec as P

MESH = pl.DeviceIdType.MESH
BF16, F32 = jnp.bfloat16, jnp.float32

base_rate = 0.5
slow_rate = 1.0
slow_beta = 0.7

PART = 80
WIDTH_PAIR = 256
M_BLOCKS = 2


def flip(v, o):
    if o == 0:
        return v
    if o == 1:
        return v + 1 - 2 * lax.rem(v, 2)
    if o == 2:
        return v + 2 - 4 * lax.div(v, 2)
    return 3 - v


class Place:
    def __init__(self):
        self.node = lax.axis_index("node")
        self.hst = lax.axis_index("hst")
        self.core = lax.rem(self.node, 2)
        self.yh = lax.div(self.node, 2)
        self.yl = lax.div(self.hst, 16)
        self.y = 2 * self.yh + self.yl
        self.oc = 1 - self.core
        self.oy = 1 - self.yh
        self.mate = (2 * self.yh + self.oc, self.hst)
        self.across = (2 * self.oy + self.core, self.hst)

    def along(self, stride):
        return lax.rem(lax.div(self.hst, stride), 4)

    def hop(self, stride, o):
        v = self.along(stride)
        return (self.node, self.hst + (flip(v, o) - v) * stride)

    def hop_y(self, o):
        other = flip(self.y, o)
        return (2 * lax.div(other, 2) + self.core, self.hst + (lax.rem(other, 2) - self.yl) * 16)


def multiple(i, size):
    return pl.ds(pl.multiple_of(i * size, size), size)


def greet(partners):
    barrier = pltpu.get_barrier_semaphore()
    for who in partners:
        pl.semaphore_signal(barrier, inc=1, device_id=who, device_id_type=MESH)
    return lambda: pl.semaphore_wait(barrier, len(partners))


def load_inputs(hid, cot, anc, mom, hv, ht, cotv, ancv, momv, in_sem, cot_sem, width, chunks):
    def load_cot(c):
        return pltpu.make_async_copy(cot.at[0, :, multiple(c, width)], cotv.at[c], cot_sem.at[c])

    load_h = pltpu.make_async_copy(hid.at[0], hv, in_sem.at[0])
    load_a = pltpu.make_async_copy(anc.at[0], ancv, in_sem.at[1])
    load_m = pltpu.make_async_copy(mom.at[0], momv, in_sem.at[2])
    load_h.start()
    load_cot(0).start()
    load_m.start()
    load_a.start()

    def start_cot(c, carry):
        load_cot(c).start()
        return carry

    lax.fori_loop(1, chunks, start_cot, 0)
    load_h.wait()

    def turn(j, carry):
        ht[multiple(j, 128), :] = hv[:, multiple(j, 128)].T
        return carry

    lax.fori_loop(0, ht.shape[0] // 128, turn, 0)
    load_m.wait()
    load_a.wait()
    return load_cot


def partial_product(c, load_cot, ht, cotv, pb, rows, width, tokens):
    load_cot(c).wait()
    scale = -base_rate / (tokens * 4)
    size = ht.shape[0] // M_BLOCKS

    def block(m, carry):
        product = jnp.dot(ht[multiple(m, size), :], cotv[c], preferred_element_type=F32)
        pb[c, m] = (product * scale).astype(BF16).reshape(2, rows, width)
        return carry

    lax.fori_loop(0, M_BLOCKS, block, 0)


def run(stages, offsets, chunks):
    def step(t, carry):
        for stage, offset in reversed(list(zip(stages, offsets))):
            c = t - offset

            @pl.when(jnp.logical_and(c >= 0, c < chunks))
            def _():
                stage(c)

        return carry

    lax.fori_loop(0, chunks + offsets[-1], step, 0)


def pair_kernel(bits, lag, chunks, width, rows,
                hid, cot, anc, mom, wout, mout,
                hv, ht, cotv, ancv, momv, pb, cr, ys, yr, st, gs, gr,
                in_sem, cot_sem, send_sem, recv_sem):
    me = Place()
    core, yh, oc, oy = me.core, me.yh, me.oc, me.oy
    far = 2 * oy + core
    partners = []
    for b in bits:
        if b == 4:
            partners.append(me.hop_y(1))
        else:
            partners.append(me.hop(1 if b < 2 else 4, 1 << b % 2))
    nb = len(bits)
    K_CORE, K_Y, K_WY, K_WC, K_WR, K_G = 0, 1, 2, 3, 4, 5
    wait_all = greet([me.mate, me.across] + partners)
    load_cot = load_inputs(hid, cot, anc, mom, hv, ht, cotv, ancv, momv, in_sem, cot_sem, width, chunks)
    wait_all()

    def remote(kind, c, src, dst, who):
        return pltpu.make_async_remote_copy(
            src_ref=src, dst_ref=dst,
            send_sem=send_sem.at[kind, lax.rem(c, send_sem.shape[1])],
            recv_sem=recv_sem.at[kind, lax.rem(c, recv_sem.shape[1])],
            device_id=who, device_id_type=MESH)

    def weights(n, c):
        return wout.at[0, multiple(n, rows), multiple(c, width)]

    def core_copy(c):
        return remote(K_CORE, c, pb.at[c, :, oc], cr.at[c], me.mate)

    def y_copy(c):
        return remote(K_Y, c, ys.at[c], yr.at[c], me.across)

    def g_copy(i, c):
        return remote(K_G + i, c, gs.at[c], gr.at[i, c], partners[i])

    def wy_copy(c):
        return remote(K_WY, c, weights(me.node, c), weights(me.node, c), me.across)

    def wc_copy(c):
        return remote(K_WC, c, weights(me.node, c), weights(me.node, c), me.mate)

    def wr_copy(c):
        return remote(K_WR, c, weights(far, c), weights(far, c), me.mate)

    def by_rows(body):
        def one(r, carry):
            body(multiple(r, 32))
            return carry

        lax.fori_loop(0, rows // 32, one, 0)

    def stage_a(c):
        partial_product(c, load_cot, ht, cotv, pb, rows, width, hid.shape[1])
        core_copy(c).start()

    def stage_b(c):
        core_copy(c).wait()

        def body(r):
            ys[c, r] = (pb[c, oy, core, r].astype(F32) + cr[c, oy, r].astype(F32)).astype(BF16)

        by_rows(body)
        y_copy(c).start()

    def stage_c(c):
        y_copy(c).wait()

        def body(r):
            grad = pb[c, yh, core, r].astype(F32) + cr[c, yh, r].astype(F32) + yr[c, r].astype(F32)
            s = ancv[r, multiple(c, width)] + grad
            st[c, r] = s
            gs[c, r] = s.astype(BF16)

        by_rows(body)
        g_copy(0, c).start()

    def stage_g(i, c):
        g_copy(i, c).wait()

        def body(r):
            s = 0.5 * (st[c, r] + gr[i, c, r].astype(F32))
            st[c, r] = s
            gs[c, r] = s.astype(BF16)

        by_rows(body)
        g_copy(i + 1, c).start()

    def stage_u(c):
        g_copy(nb - 1, c).wait()

        def body(r):
            s = 0.5 * (st[c, r] + gr[nb - 1, c, r].astype(F32))
            a = ancv[r, multiple(c, width)]
            new = slow_beta * momv[r, multiple(c, width)] + (a - s) / base_rate
            mout[0, r, multiple(c, width)] = new
            here = pl.ds(pl.multiple_of(me.node * rows + r.start, 32), 32)
            wout[0, here, multiple(c, width)] = (a - slow_rate * base_rate * new).astype(BF16)

        by_rows(body)
        wy_copy(c).start()
        wc_copy(c).start()

    def stage_r(c):
        wy_copy(c).wait()
        wc_copy(c).wait()
        wr_copy(c).start()

    def stage_z(c):
        wr_copy(c).wait()

    stages = [stage_a, stage_b, stage_c]
    stages += [functools.partial(stage_g, i) for i in range(nb - 1)]
    stages += [stage_u, stage_r, stage_z]
    run(stages, [lag * i for i in range(len(stages))], chunks)


def ring_kernel(stride, group, extra, lag, chunks, width, rows,
                hid, cot, anc, mom, wout, mout,
                hv, ht, cotv, ancv, momv, pb, cr, sq, r1, st, es, er, sy, ry, av, ms, mr,
                in_sem, cot_sem, send_sem, recv_sem):
    me = Place()
    core, yh, oc, oy, y = me.core, me.yh, me.oc, me.oy, me.y
    n = len(group) + 1
    part_w = width // n
    v = me.along(stride)
    members = (lambda o: flip(v, o)) if n == 4 else (lambda o: lax.rem(lax.div(flip(v, o), group[0]), 2))
    own = members(0)
    ne = len(extra)
    first = [me.hop(stride, o) for o in group]
    swaps = [me.hop(s, o) for s, o in extra]
    ring = [me.hop_y(o) for o in (1, 2, 3)]
    hosts = 2 * n * 2**ne
    K_CORE, K_M, K_WC = 0, 1, 2
    K_R = 3
    K_E = K_R + n - 1
    K_Y = K_E + ne
    K_AY = K_Y + 3
    K_AR = K_AY + 3
    wait_all = greet([me.mate] + first + swaps + ring)
    load_cot = load_inputs(hid, cot, anc, mom, hv, ht, cotv, ancv, momv, in_sem, cot_sem, width, chunks)
    wait_all()

    def remote(kind, c, src, dst, who):
        return pltpu.make_async_remote_copy(
            src_ref=src, dst_ref=dst,
            send_sem=send_sem.at[kind, lax.rem(c, send_sem.shape[1])],
            recv_sem=recv_sem.at[kind, lax.rem(c, recv_sem.shape[1])],
            device_id=who, device_id_type=MESH)

    def core_copy(c):
        return remote(K_CORE, c, pb.at[c, :, oc], cr.at[c], me.mate)

    def mom_copy(c):
        return remote(K_M, c, ms.at[c], mr.at[c], me.across)

    def r_copy(i, c):
        return remote(K_R + i, c, sq.at[c, members(group[i])], r1.at[c, i], first[i])

    def e_copy(i, c):
        return remote(K_E + i, c, es.at[c], er.at[i, c], swaps[i])

    def y_copy(i, c):
        return remote(K_Y + i, c, sy.at[c, flip(y, i + 1)], ry.at[c, i], ring[i])

    def ay_copy(i, c):
        return remote(K_AY + i, c, av.at[c, own, y], av.at[c, own, y], ring[i])

    def ar_copy(i, c):
        return remote(K_AR + i, c, av.at[c, own], av.at[c, own], first[i])

    def weights(h, c):
        return wout.at[0, multiple(2 * h + core, rows), multiple(c, width)]

    def wc_copy(h, c):
        return remote(K_WC + (K_AR + n - 1 - K_WC) * h, c, weights(h, c), weights(h, c), me.mate)

    def quarters(body):
        def one(q, carry):
            body(q)
            return carry

        lax.fori_loop(0, 4, one, 0)

    def stage_a(c):
        partial_product(c, load_cot, ht, cotv, pb, rows, width, hid.shape[1])
        core_copy(c).start()

        def body(r, carry):
            ms[c, multiple(r, PART)] = momv[multiple(r, PART), multiple(c, width)].astype(BF16)
            return carry

        lax.fori_loop(0, 2, body, 0)
        mom_copy(c).start()

    def stage_b(c):
        core_copy(c).wait()
        mom_copy(c).wait()

        def body(q):
            h, r = lax.div(q, 2), multiple(lax.rem(q, 2), PART)
            s = pb[c, h, core, r].astype(F32) + cr[c, h, r].astype(F32)
            s = s + jnp.where(h == yh, ancv[r, multiple(c, width)], 0.0)
            s = s.astype(BF16)
            for j in range(n):
                sq[c, j, q] = s[:, j * part_w:(j + 1) * part_w]

        quarters(body)
        for i in range(n - 1):
            r_copy(i, c).start()

    def send_on(i, c):
        if i < ne:
            e_copy(i, c).start()
        else:
            for o in range(3):
                y_copy(o, c).start()

    def keep(i, c, q, s):
        if i < ne:
            st[c, q] = s
            es[c, q] = s.astype(BF16)
        else:
            sy[c, q] = s.astype(BF16)

    def stage_r(c):
        for i in range(n - 1):
            r_copy(i, c).wait()

        def body(q):
            s = sq[c, own, q].astype(F32)
            for i in range(n - 1):
                s = s + r1[c, i, q].astype(F32)
            keep(0, c, q, s)

        quarters(body)
        send_on(0, c)

    def stage_e(i, c):
        e_copy(i, c).wait()
        quarters(lambda q: keep(i + 1, c, q, st[c, q] + er[i, c, q].astype(F32)))
        send_on(i + 1, c)

    def stage_f(c):
        for i in range(3):
            y_copy(i, c).wait()
        s = sy[c, y].astype(F32) + ry[c, 0].astype(F32) + ry[c, 1].astype(F32) + ry[c, 2].astype(F32)
        av[c, own, y] = (s * (1.0 / hosts)).astype(BF16)
        for i in range(3):
            ay_copy(i, c).start()

    def stage_g(c):
        for i in range(3):
            ay_copy(i, c).wait()
        for i in range(n - 1):
            ar_copy(i, c).start()

    def stage_u(c):
        for i in range(n - 1):
            ar_copy(i, c).wait()

        def body(p, carry):
            r = multiple(p, PART)
            for j in range(n):
                w = pl.ds(pl.multiple_of(c * width + j * part_w, part_w), part_w)
                a = ancv[r, w]
                new = slow_beta * momv[r, w] + (a - av[c, j, 2 * yh + p].astype(F32)) / base_rate
                mout[0, r, w] = new
                here = pl.ds(pl.multiple_of((2 * yh + core) * rows + p * PART, PART), PART)
                there = pl.ds(pl.multiple_of((2 * oy + core) * rows + p * PART, PART), PART)
                wout[0, here, w] = (a - slow_rate * base_rate * new).astype(BF16)
                shift = mr[c, r, pl.ds(j * part_w, part_w)].astype(F32) * (slow_rate * base_rate * slow_beta)
                wout[0, there, w] = (av[c, j, 2 * oy + p].astype(F32) - shift).astype(BF16)
            return carry

        lax.fori_loop(0, 2, body, 0)
        wc_copy(0, c).start()
        wc_copy(1, c).start()

    def stage_z(c):
        wc_copy(0, c).wait()
        wc_copy(1, c).wait()

    stages = [stage_a, stage_b, stage_r]
    stages += [functools.partial(stage_e, i) for i in range(ne)]
    stages += [stage_f, stage_g, stage_u, stage_z]
    run(stages, [lag * i for i in range(len(stages))], chunks)


def outer_step(mask, hidden, cotangent, anchor, momentum):
    tokens, h = hidden.shape[1:]
    d = cotangent.shape[2]
    rows = anchor.shape[1]
    dma = pltpu.SemaphoreType.DMA
    lowest = mask & 15
    if mask & 16 and lowest:
        z, x = mask & 3, mask >> 2 & 3
        stride, value, other, rest = (4, x, 1, z) if x == 3 or not z or (z != 3 and x) else (1, z, 4, x)
        group = (1, 2, 3) if value == 3 else (value,)
        extra = [(other, o) for o in (1, 2) if rest & o]
        n, ne = len(group) + 1, len(extra)
        width = 128 * max(n, 2)
        chunks = d // width
        lag = 3 if n == 2 else 2
        part_w = width // n
        piece = (4, PART, part_w)
        body = functools.partial(ring_kernel, stride, group, extra, lag, chunks, width, rows)
        kinds = 3 + 2 * (n - 1) + ne + 6 + 1
        scratch = [
            pltpu.VMEM((chunks, n) + piece, BF16),
            pltpu.VMEM((chunks, n - 1) + piece, BF16),
            pltpu.VMEM((chunks if ne else 1,) + piece, F32),
            pltpu.VMEM((chunks if ne else 1,) + piece, BF16),
            pltpu.VMEM((max(ne, 1), chunks if ne else 1) + piece, BF16),
            pltpu.VMEM((chunks,) + piece, BF16),
            pltpu.VMEM((chunks, 3, PART, part_w), BF16),
            pltpu.VMEM((chunks, n) + piece, BF16),
            pltpu.VMEM((chunks, rows, width), BF16),
            pltpu.VMEM((chunks, rows, width), BF16),
        ]
    else:
        bits = [b for b in range(5) if mask >> b & 1]
        nb = len(bits)
        width = WIDTH_PAIR
        chunks = d // width
        lag = 3 if nb <= 2 else 2
        block = (chunks, rows, width)
        body = functools.partial(pair_kernel, bits, lag, chunks, width, rows)
        kinds = 5 + nb
        scratch = [
            pltpu.VMEM(block, BF16),
            pltpu.VMEM(block, BF16),
            pltpu.VMEM(block, F32),
            pltpu.VMEM(block, BF16),
            pltpu.VMEM((nb,) + block, BF16),
        ]
    return pl.pallas_call(
        body,
        out_shape=(jax.ShapeDtypeStruct((1, h, d), BF16), jax.ShapeDtypeStruct((1, rows, d), F32)),
        in_specs=[pl.BlockSpec(memory_space=pltpu.HBM)] * 4,
        out_specs=[pl.BlockSpec(memory_space=pltpu.VMEM)] * 2,
        scratch_shapes=[
            pltpu.VMEM((tokens, h), BF16),
            pltpu.VMEM((h, tokens), BF16),
            pltpu.VMEM((chunks, tokens, width), BF16),
            pltpu.VMEM((rows, d), F32),
            pltpu.VMEM((rows, d), F32),
            pltpu.VMEM((chunks, 2, 2, rows, width), BF16),
            pltpu.VMEM((chunks, 2, rows, width), BF16),
        ] + scratch + [
            dma((3,)),
            dma((chunks,)),
            dma((kinds, lag)),
            dma((kinds, 2 * lag)),
        ],
        compiler_params=pltpu.CompilerParams(
            collective_id=mask, has_side_effects=True, vmem_limit_bytes=VMEM_LIMIT),
        name=f"outer_{mask}",
    )(hidden, cotangent, anchor, momentum)


VMEM_LIMIT = 54 * 1024 * 1024
MASKS = range(1, 32)


def local(hidden, cotangent, anchor, momentum, round_mask):
    branches = [functools.partial(outer_step, mask) for mask in MASKS]
    return lax.switch(round_mask[0] - 1, branches, hidden, cotangent, anchor, momentum)


def solution(mesh):
    placed = (
        P("hst", "node", None),
        P("hst", "node", None),
        P("hst", "node", None),
        P("hst", "node", None),
        P(),
    )
    return jax.shard_map(
        local,
        mesh=mesh,
        in_specs=placed,
        out_specs=(P("hst", None, None), P("hst", "node", None)),
        check_vma=False,
    )
```

time: 319 us -> 126 us (0.39)
  waiting for transfers between devices: 269 us -> 0 us
  Pallas kernels: 0 us -> 110 us
  between operations: 14.7 us -> 1.29 us
  matrix products: 10.5 us -> 0 us
  starting transfers between devices: 8.68 us -> 0 us
  other arithmetic: 8.62 us -> 0 us
  loops' own time: 0 us -> 7.25 us
    ppermute x5 -> x0, waiting for transfers between devices: 151 us -> none  [swapped(): return lax.ppermute(block, axis, route)]
    pallas_call x0 -> x1, Pallas kernels: none -> 110 us  [outer_step(): pl.pallas_call(body, out_shape=(jax.ShapeDtypeStruct((1, h, d), BF16), ja...]
    reduce_scatter x1 -> x0, waiting for transfers between devices: 66 us -> none  [local(): lax.psum_scatter((product * token_scale).astype(jnp.bfloat16), 'node', sc...]
    all_gather x1 -> x0, waiting for transfers between devices: 52.7 us -> none  [local(): weights_whole = lax.all_gather(updated[None], 'node', axis=1, tiled=True)]
    dot_general x1 -> x0, matrix products: 10.5 us -> none  [local(): lax.dot_general(tokens_here, grads_in, (((0,), (0,)), ((), ())), preferre...]
    convert_element_type x6 -> x0, other arithmetic: 8.62 us -> none  [the longest x5 5.16 us: half_step(): current.astype(jnp.bfloat16)]
    ppermute x5 -> x0, starting transfers between devices: 8.6 us -> none  [swapped(): return lax.ppermute(block, axis, route)]
    another operation x0 -> x1, loops' own time: none -> 7.25 us  [local(): lax.switch(round_mask[0] - 1, branches, hidden, cotangent, anchor, momentum)]
  transfers between devices with their start and end apart: 7 -> 0, of which waited for: 7 -> 0; matrix products, arithmetic and copies ran while one was open for 0% -> 0% of each run, Pallas kernels for 0% -> 0%
where the time goes in v1:
time: 126 us
  Pallas kernels  110 us (87%)
  loops' own time  7.25 us (6%)
  local copies, waits for them, and re-layouts  7.22 us (6%)
  between operations  1.29 us (1%)
    pallas_call x1, Pallas kernels, outer_step(): pl.pallas_call(body, out_shape=(jax.ShapeDtypeStruct((1, h, d), BF16), ja...  110 us
    another operation x1, loops' own time, local(): lax.switch(round_mask[0] - 1, branches, hidden, cotangent, anchor, momentum)  7.25 us
    unnamed x2, local copies, waits for them, and re-layouts  7.22 us

profile of v1, /device:TPU:1, one launch (start us, length us, event | category | flops | bytes accessed | tf_op | source)
XLA Modules:
  0.0 125.6 jit_solution(17876910641753347944)
XLA Ops:
  1.3 117.1 %conditional.1 = ((bf16[1,640,4608]{2,1,0:T(8,128)(2,1)}, f32[1,160,4608]{2,1,0:T(8,128)S(1)})) conditional(s32[]{:T(128)} %bitcast, (bf16[1,1024,640]{2,1,0:T(8,128)(2,1)}, bf16[1,1024,4608]{2,1,0:T(8,128)(2,1)}, f32[1,160,4608]{2,1,0:T(8,128)}, f32[1,160,4608]{2,1,0:T(8,128)}) %tuple.100, ...), branch_computations={%region_0.0_spmd, %region_1.0_spmd, %region_2.0_spmd, %region_3.0_... | conditional | bytes 8 | solution.py:493
  1.3 109.8 %outer_16.1 = (bf16[1,640,4608]{2,1,0:T(8,128)(2,1)}, f32[1,160,4608]{2,1,0:T(8,128)S(1)}) custom-call(bf16[1,1024,640]{2,1,0:T(8,128)(2,1)} %get-tuple-element.308.hid, bf16[1,1024,4608]{2,1,0:T(8,128)(2,1)} %get-tuple-element.309.cot, f32[1,160,4608]{2,1,0:T(8,128)} %get-tuple-element.310.anc, f32[1,160,4608]{2,1,0:T(8,128)} %get-tuple-element.311.mom), custom_call_target="tpu_custom_call" | custom-call | tf_op jit(solution)/shard_map/cond/branch_15_fun/outer_16/pallas_call | solution.py:462
  118.4 5.6 %copy.134 = bf16[1,640,4608]{2,1,0:T(8,128)(2,1)} copy(bf16[1,640,4608]{2,1,0:T(8,128)(2,1)} %get-tuple-element.502) | data formatting | bytes 11796480
  124.0 1.6 %copy.135 = f32[1,160,4608]{2,1,0:T(8,128)} copy(f32[1,160,4608]{2,1,0:T(8,128)S(1)} %get-tuple-element.503) | data formatting | bytes 5898240
